TPU v7x, 32 devices: a whole 2x2x4 slice. The times are simulated.
32 devices in a mesh: groups: 2 (over x), dp: 2 (over core), tensor: 8 (over z, y).
Axes of the slice: x: 2, y: 2, z: 4, core: 2. Of those that a mesh axis runs over, the one named last changes fastest.
Arguments:
- reward_hidden: bfloat16 [32, 256, 8192], P(('groups', 'dp'), None, 'tensor'), parts along dimension 0, may hold values from -6 to 6
- reward_gain: float32 [8192], P('tensor'), may hold values from 0.5 to 1.5
- reward_head: float32 [8192], P('tensor'), may hold values from -1 to 1
- decode_inputs: bfloat16 [2, 32, 8192], P(None, ('groups', 'dp'), 'tensor'), parts along dimension 1, may hold values from -6 to 6
- attn_gain: float32 [8192], replicated, may hold values from 0.5 to 1.5
- w_query: bfloat16 [8192, 8192], P(None, 'tensor'), may hold values from -0.0625 to 0.0625
- w_keyval: bfloat16 [8192, 2048], P(None, 'tensor'), may hold values from -0.0625 to 0.0625
- w_out: bfloat16 [8192, 8192], P('tensor'), may hold values from -3 to 3
- cache_keys: bfloat16 [32, 2048, 1024], P(('groups', 'dp'), 'tensor'), parts along dimension 0, may hold values from -720 to 720
- cache_values: bfloat16 [32, 2048, 1024], P(('groups', 'dp'), 'tensor'), parts along dimension 0, may hold values from -6 to 6
- lengths: int32 [32], P('groups'), parts along dimension 0, may hold values from 512 to 2048
- slot_map: int32 [32], P('groups'), parts along dimension 0, may hold values from 0 to 15, as said below
Outputs:
- reward: float32 [32], P(('groups', 'dp')), parts along dimension 0
- decoded: bfloat16 [2, 32, 8192], P(None, ('groups', 'dp'), 'tensor'), parts along dimension 1
There are 2 independent parts, one for each index of `groups`. A program takes and returns all parts, laid end to end along the dimension named above; an argument that names none is the same for every part. Nothing has to cross between parts.
Inputs may be any that keep to these rules, and one draw needn't show every extreme that they name: `slot_map`: each aligned block of 8 slots holds exactly 4 survivors, which map to themselves; every other slot maps to a survivor, and every survivor is named by exactly one other slot.
All inputs are finite; a program needn't handle non-finite values.
Results may differ from a plain program's by a relative error of at most 0.0055.
The roundings to bfloat16 on the way count: a program that leaves them out, or rounds other values in their place, can miss the bound.
Values may be sent and summed in bfloat16 or wider, within the bound.
No kernel may reach another device: no remote copies, remote signals or barrier semaphores. Data moves between devices by JAX's collectives and lax.ppermute only.
A program may use at most 128 MiB of HBM per device.

v0:
```python
import jax
import jax.numpy as jnp
from jax import lax
from jax.sharding import PartitionSpec as P

D = 8192
QH = 64
KVH = 8
HD = 128
STEPS = 2
EPS = 1e-05
NEG = -1e30


def fold_sources(parts):
    maxima, totals, sums = parts
    top = jnp.max(maxima, axis=0)
    factor = jnp.exp(maxima - top[None])
    return (top, jnp.sum(factor * totals, axis=0), jnp.sum(factor[..., None] * sums, axis=0))


def local(
    reward_hidden,
    reward_gain,
    reward_head,
    decode_inputs,
    attn_gain,
    w_query,
    w_keyval,
    w_out,
    cache_keys,
    cache_values,
    lengths,
    slot_map,
):
    hidden = reward_hidden.astype(jnp.float32)
    squares = jnp.sum(hidden * hidden, axis=-1)
    head_dot = jnp.sum(hidden * (reward_gain * reward_head), axis=-1)
    squares, head_dot = lax.psum((squares, head_dot), "tensor")
    reward = jnp.mean(head_dot * lax.rsqrt(squares / D + EPS), axis=-1)
    rows = cache_keys.shape[0]
    width = cache_keys.shape[1]
    base = lax.axis_index("dp") * rows
    mine = lax.dynamic_slice_in_dim(slot_map, base, rows)
    every_k, every_v = (
        lax.all_gather(cache_keys, "dp", axis=0, tiled=True),
        lax.all_gather(cache_values, "dp", axis=0, tiled=True),
    )
    keys_now = jnp.take(every_k, mine, axis=0)
    values_now = jnp.take(every_v, mine, axis=0)
    live = jnp.take(lengths, mine, axis=0)
    group = QH // KVH
    heads_dev = w_query.shape[1] // HD
    keys4 = keys_now.reshape(rows, width, KVH, HD)
    values4 = values_now.reshape(rows, width, KVH, HD)
    positions = lax.axis_index("tensor") * width + jnp.arange(width)
    valid = (positions[None, :] < live[:, None])[:, None, None, :]
    head_start = lax.axis_index("tensor") * heads_dev
    kv_index = (head_start + jnp.arange(heads_dev)) // group
    scale = HD ** (-0.5)
    new_keys = []
    new_values = []
    outputs = []
    for step in range(STEPS):
        whole = lax.all_gather(decode_inputs[step], "tensor", axis=1, tiled=True).astype(
            jnp.float32
        )
        normed = (
            whole * lax.rsqrt(jnp.mean(whole * whole, axis=-1, keepdims=True) + EPS) * attn_gain
        ).astype(jnp.bfloat16)
        query_part = jnp.dot(normed, w_query, preferred_element_type=jnp.float32).astype(
            jnp.bfloat16
        )
        kv_part = jnp.dot(normed, w_keyval, preferred_element_type=jnp.float32).astype(jnp.bfloat16)
        query_all, keyval = (
            lax.all_gather(query_part, "tensor", axis=1, tiled=True),
            lax.all_gather(kv_part, "tensor", axis=1, tiled=True),
        )
        query = query_all.reshape(rows, KVH, group, HD)
        keyval = keyval.reshape(rows, 2, KVH, HD)
        new_keys.append(keyval[:, 0])
        new_values.append(keyval[:, 1])
        scores = (
            jnp.einsum("rkgd,rwkd->rkgw", query, keys4, preferred_element_type=jnp.float32) * scale
        )
        scores = jnp.where(valid, scores, NEG)
        block_max = jnp.max(scores, axis=-1)
        expo = jnp.where(valid, jnp.exp(scores - block_max[..., None]), 0.0)
        block_total = jnp.sum(expo, axis=-1).reshape(rows, QH)
        block_acc = jnp.einsum(
            "rkgw,rwkd->rkgd",
            expo.astype(jnp.bfloat16),
            values4,
            preferred_element_type=jnp.float32,
        )
        block_acc = block_acc.reshape(rows, QH, HD)
        block_max = block_max.reshape(rows, QH)
        cache_top, cache_total, cache_acc = fold_sources(
            (
                lax.all_to_all(block_max[None], "tensor", split_axis=2, concat_axis=0, tiled=True),
                lax.all_to_all(
                    block_total[None], "tensor", split_axis=2, concat_axis=0, tiled=True
                ),
                lax.all_to_all(block_acc[None], "tensor", split_axis=2, concat_axis=0, tiled=True),
            )
        )
        query_own = query_part.reshape(rows, heads_dev, HD)
        fresh_k = jnp.take(jnp.stack(new_keys, axis=1), kv_index, axis=2)
        fresh_v = jnp.take(jnp.stack(new_values, axis=1), kv_index, axis=2)
        recent = (
            jnp.einsum("rhd,rjhd->rhj", query_own, fresh_k, preferred_element_type=jnp.float32)
            * scale
        )
        recent_max = jnp.max(recent, axis=-1)
        recent_exp = jnp.exp(recent - recent_max[..., None])
        recent_total = jnp.sum(recent_exp, axis=-1)
        recent_acc = jnp.einsum(
            "rhj,rjhd->rhd",
            recent_exp.astype(jnp.bfloat16),
            fresh_v,
            preferred_element_type=jnp.float32,
        )
        top = jnp.maximum(cache_top, recent_max)
        cache_factor = jnp.exp(cache_top - top)
        recent_factor = jnp.exp(recent_max - top)
        total = cache_factor * cache_total + recent_factor * recent_total
        acc = cache_factor[..., None] * cache_acc + recent_factor[..., None] * recent_acc
        attended = (acc / total[..., None]).astype(jnp.bfloat16).reshape(rows, heads_dev * HD)
        partial_out = jnp.dot(attended, w_out, preferred_element_type=jnp.float32)
        summed = lax.psum_scatter(partial_out, "tensor", scatter_dimension=1, tiled=True)
        outputs.append(summed.astype(jnp.bfloat16))
    return (reward, jnp.stack(outputs, axis=0))


def solution(mesh):
    return jax.shard_map(
        local,
        mesh=mesh,
        in_specs=(
            P(("groups", "dp"), None, "tensor"),
            P("tensor"),
            P("tensor"),
            P(None, ("groups", "dp"), "tensor"),
            P(),
            P(None, "tensor"),
            P(None, "tensor"),
            P("tensor", None),
            P(("groups", "dp"), "tensor", None),
            P(("groups", "dp"), "tensor", None),
            P("groups"),
            P("groups"),
        ),
        out_specs=(P(("groups", "dp")), P(None, ("groups", "dp"), "tensor")),
        check_vma=False,
    )
```

profile of v0, /device:TPU:0, one launch (start us, length us, event | category | flops | bytes accessed | tf_op | source)
XLA Modules:
  0.0 486.0 jit_solution(13673014890106930044)
XLA Ops:
  8.7 32.3 %all-gather = bf16[1,8,8192]{2,1,0:T(8,128)(2,1)S(1)} all-gather(bf16[1,8,1024]{2,1,0:T(8,128)(2,1)S(1)} %get-tuple-element.26), channel_id=2, replica_groups=mesh['groups'=2,'dp'=2,'tensor'=8] {'tensor'}, dimensions={2}, use_global_device_ids=true | all-gather | bytes 147456 | tf_op jit(solution)/shard_map/all_gather | solution.py:65
  41.2 3.5 convolution_convert_fusion.3
  44.8 30.6 %all_gather.27 = bf16[8,2048]{1,0:T(8,128)(2,1)S(1)} all-gather(bf16[8,256]{1,0:T(8,128)(2,1)S(1)} %convolution_convert_fusion.3), channel_id=1, replica_groups=mesh['groups'=2,'dp'=2,'tensor'=8] {'tensor'}, dimensions={1}, use_global_device_ids=true | all-gather | bytes 36864 | tf_op jit(solution)/shard_map/all_gather | solution.py:77
  76.0 8.2 %fusion.61 = (f32[8,8]{0,1:T(8,128)S(1)}, bf16[8,1024]{1,0:T(8,128)(2,1)S(1)}) fusion(bf16[8,8,128]{2,1,0:T(8,128)(2,1)S(1)} %gather_fusion.2, pred[8]{0:T(512)(128)(4,1)S(1)} %compare_and_fusion, bf16[8192,1024]{1,0:T(8,128)(2,1)} %param.23, bf16[1,8,8192]{2,1,0:T(8,128)(2,1)S(1)} %all-gather, f32[8192]{0:T(1024)S(1)} %copy-done.2, f32[8]{0:T(128)S(1)} %add_rsqrt_fusion.1), kind=kOutput, calls=%fused_computation.78 | convolution fusion | flops 134528960 | bytes 16974120 | tf_op jit(solution)/shard_map/dot_general | solution.py:71
  84.8 30.5 %all-gather.1 = bf16[1,8,8192]{2,1,0:T(8,128)(2,1)S(1)} all-gather(bf16[1,8,1024]{2,1,0:T(8,128)(2,1)S(1)} %get-tuple-element.27), channel_id=3, replica_groups=mesh['groups'=2,'dp'=2,'tensor'=8] {'tensor'}, dimensions={2}, use_global_device_ids=true | all-gather | bytes 147456 | tf_op jit(solution)/shard_map/all_gather | solution.py:65
  118.4 30.6 %all_gather.31 = bf16[8,2048]{1,0:T(8,128)(2,1)S(1)} all-gather(bf16[8,256]{1,0:T(8,128)(2,1)S(1)} %convolution_convert_fusion.2), channel_id=1, replica_groups=mesh['groups'=2,'dp'=2,'tensor'=8] {'tensor'}, dimensions={1}, use_global_device_ids=true | all-gather | bytes 36864 | tf_op jit(solution)/shard_map/all_gather | solution.py:77
  150.3 8.1 %convolution_convert_fusion = bf16[8,1024]{1,0:T(8,128)(2,1)S(1)} fusion(bf16[8192,1024]{1,0:T(8,128)(2,1)} %param.23, bf16[1,8,8192]{2,1,0:T(8,128)(2,1)S(1)} %all-gather.1, f32[8]{0:T(128)S(1)} %add_rsqrt_fusion, f32[8192]{0:T(1024)S(1)} %copy-done.2), kind=kOutput, calls=%fused_computation.31 | convolution fusion | flops 134488064 | bytes 16957472 | tf_op jit(solution)/shard_map/dot_general | solution.py:71
  159.8 3.6 fusion.1
  163.5 37.1 %all-reduce = (f32[8,256]{1,0:T(8,128)S(1)}, f32[8,256]{1,0:T(8,128)S(1)}) all-reduce(f32[8,256]{1,0:T(8,128)S(1)} %get-tuple-element.6, f32[8,256]{1,0:T(8,128)S(1)} %get-tuple-element.4), channel_id=1, replica_groups=mesh['groups'=2,'dp'=2,'tensor'=8] {'tensor'}, use_global_device_ids=true, to_apply=%region_1.0 | all-reduce | flops 4096 | bytes 32768 | tf_op jit(solution)/shard_map/psum | solution.py:39
  200.5 30.5 %all_gather.30 = bf16[8,8192]{1,0:T(8,128)(2,1)S(1)} all-gather(bf16[8,1024]{1,0:T(8,128)(2,1)S(1)} %convolution_convert_fusion), channel_id=1, replica_groups=mesh['groups'=2,'dp'=2,'tensor'=8] {'tensor'}, dimensions={1}, use_global_device_ids=true | all-gather | bytes 147456 | tf_op jit(solution)/shard_map/all_gather | solution.py:76
  231.0 30.7 %all_gather.25 = bf16[8,8192]{1,0:T(8,128)(2,1)S(1)} all-gather(bf16[8,1024]{1,0:T(8,128)(2,1)S(1)} %get-tuple-element.43), channel_id=1, replica_groups=mesh['groups'=2,'dp'=2,'tensor'=8] {'tensor'}, dimensions={1}, use_global_device_ids=true | all-gather | bytes 147456 | tf_op jit(solution)/shard_map/all_gather | solution.py:76
  262.0 6.1 %gather_fusion.1 = bf16[8,256,1024]{2,1,0:T(8,128)(2,1)} fusion(bf16[16,256,1024]{2,1,0:T(8,128)(2,1)} %all-gather.5.cloned.1.call-done, s32[1024]{0:T(1024)S(1)} %pad_clamp_fusion.1), kind=kCustom, calls=%fused_computation.clone | custom fusion | bytes 8388640 | tf_op jit(solution)/shard_map/jit(_take)/gather | solution.py:49
  268.2 6.2 %gather_fusion.3 = bf16[8,256,1024]{2,1,0:T(8,128)(2,1)} fusion(bf16[16,256,1024]{2,1,0:T(8,128)(2,1)} %all-gather.7.cloned.1.call-done, s32[1024]{0:T(1024)S(1)} %pad_clamp_fusion.1), kind=kCustom, calls=%fused_computation.3.clone | custom fusion | bytes 8388640 | tf_op jit(solution)/shard_map/jit(_take)/gather | solution.py:50
  274.3 6.2 %select_bitcast_fusion.1 = (bf16[8,32,8,8,128]{4,3,2,1,0:T(8,128)(2,1)S(1)}, bf16[8,32,8,8,128]{4,3,2,1,0:T(8,128)(2,1)}) fusion(bf16[8,256,1024]{2,1,0:T(8,128)(2,1)} %gather_fusion.1, pred[8]{0:T(512)(128)(4,1)S(1)} %get-tuple-element.18, bf16[8,256,1024]{2,1,0:T(8,128)(2,1)} %gather_fusion.3), kind=kLoop, calls=%fused_computation.20 | loop fusion | flops 4194304 | bytes 16777224
  303.9 5.4 %all-to-all-start.5 = ((f32[1,8,64]{1,0,2:T(1,128)}), f32[1,8,64]{1,0,2:T(1,128)S(1)}, u32[]{:S(2)}, u32[]{:S(2)}) async-start(f32[1,8,64]{1,0,2:T(1,128)} %bitcast.47), calls=%async_computation.6 | async-start | bytes 65536 | tf_op jit(solution)/shard_map/all_to_all | solution.py:101
  309.4 6.6 %all-to-all-done.5 = f32[1,8,64]{1,0,2:T(1,128)S(1)} async-done(((f32[1,8,64]{1,0,2:T(1,128)}), f32[1,8,64]{1,0,2:T(1,128)S(1)}, u32[]{:S(2)}, u32[]{:S(2)}) %all-to-all-start.5) | async-done | bytes 2080 | tf_op jit(solution)/shard_map/all_to_all | solution.py:101
  319.4 6.6 %all-to-all-done.3 = f32[1,8,64]{1,0,2:T(1,128)S(1)} async-done(((f32[1,8,64]{1,0,2:T(1,128)}), f32[1,8,64]{1,0,2:T(1,128)S(1)}, u32[]{:S(2)}, u32[]{:S(2)}) %all-to-all-start.3) | async-done | bytes 2080 | tf_op jit(solution)/shard_map/all_to_all | solution.py:100
  325.9 3.4 all-to-all-start.1
  329.7 7.8 %all-to-all-done.1 = f32[1,8,64,128]{3,1,0,2:T(8,128)S(1)} async-done(((f32[1,8,64,128]{3,1,0,2:T(8,128)}), f32[1,8,64,128]{3,1,0,2:T(8,128)S(1)}, u32[]{:S(2)}, u32[]{:S(2)}) %all-to-all-start.1) | async-done | bytes 262176 | tf_op jit(solution)/shard_map/all_to_all | solution.py:104
  337.5 3.4 all-to-all-start.4
  341.1 8.8 %fusion.75 = f32[8,8192]{1,0:T(8,128)} fusion(bf16[1024,8192]{1,0:T(8,128)(2,1)} %param.25, f32[8,8,128]{2,1,0:T(8,128)S(1)} %fusion.44, bf16[8,8,128]{2,1,0:T(8,128)(2,1)S(1)} %gather_fusion.4, f32[8,8]{0,1:T(8,128)S(1)} %copy.125, f32[8,8]{0,1:T(8,128)S(1)} %copy.122, f32[8,8]{0,1:T(8,128)S(1)} %copy.121, f32[8,8]{0,1:T(8,128)S(1)} %copy.116, ...), kind=kOutput, calls=%fused_computation.96 | convolution fusion | flops 134283264 | bytes 17089544 | tf_op jit(solution)/shard_map/dot_general | solution.py:129
  350.2 8.8 %fusion.73 = f32[8,8192]{1,0:T(8,128)} fusion(bf16[1024,8192]{1,0:T(8,128)(2,1)} %param.25, f32[8,8,1,128]{3,2,1,0:T(1,128)S(1)} %fusion.63, f32[8,8,128]{2,0,1:T(8,128)S(1)} %multiply_reduce_fusion, f32[8,8]{0,1:T(8,128)S(1)} %get-tuple-element.13, f32[8,8]{0,1:T(8,128)S(1)} %get-tuple-element.15, f32[8,8]{0,1:T(8,128)S(1)} %get-tuple-element.14), kind=kOutput, calls=%fused_computation.94 | convolution fusion | flops 134258688 | bytes 17105664 | tf_op jit(solution)/shard_map/dot_general | solution.py:129
  359.6 53.8 %reduce-scatter.3.cloned.1.call-done = f32[8,1024]{1,0:T(8,128)} async-done(((f32[8,8192]{1,0:T(8,128)}), f32[8,1024]{1,0:T(8,128)}) %reduce-scatter.3.cloned.1.call-update) | async-done | bytes 32784 | tf_op jit(solution)/shard_map/reduce_scatter | solution.py:130
  414.2 63.9 %reduce-scatter.5.cloned.1.call-done = f32[8,1024]{1,0:T(8,128)} async-done(((f32[8,8192]{1,0:T(8,128)}), f32[8,1024]{1,0:T(8,128)}) %reduce-scatter.5.cloned.1.call-update) | async-done | bytes 32784 | tf_op jit(solution)/shard_map/reduce_scatter | solution.py:130
  (93 shorter events, 39.1 us)
Async XLA Ops:
  7.2 152.0 %copy-start = (s32[16]{0:T(128)S(1)}, s32[16]{0:T(128)}, u32[]{:S(2)}) copy-start(s32[16]{0:T(128)} %param.28) | copy-start | bytes 196
  7.2 1.5 copy-start.3
  7.2 34.1 %copy-start.2 = (f32[8192]{0:T(1024)S(1)}, f32[8192]{0:T(1024)}, u32[]{:S(2)}) copy-start(f32[8192]{0:T(1024)} %param.22) | copy-start | bytes 98308
  7.2 254.8 %all-gather.5.cloned.1.call-start = ((), (), s32[]{:S(2)}) async-start(), calls=%async_computation.8 | async-start | bytes 12582912 | tf_op jit(solution)/shard_map/all_gather | solution.py:46
  7.9 260.2 %all-gather.7.cloned.1.call-start = ((), (), s32[]{:S(2)}) async-start(), calls=%async_computation.9 | async-start | bytes 12582912 | tf_op jit(solution)/shard_map/all_gather | solution.py:47
  150.3 8.8 %copy-start.6 = (s32[16]{0:T(128)S(1)}, s32[16]{0:T(128)}, u32[]{:S(2)}) copy-start(s32[16]{0:T(128)} %param.29) | copy-start | bytes 196
  150.3 9.5 %copy-start.4 = (f32[1024]{0:T(1024)S(1)}, f32[1024]{0:T(1024)}, u32[]{:S(2)}) copy-start(f32[1024]{0:T(1024)} %param.19) | copy-start | bytes 12292
  150.3 9.5 %copy-start.5 = (f32[1024]{0:T(1024)S(1)}, f32[1024]{0:T(1024)}, u32[]{:S(2)}) copy-start(f32[1024]{0:T(1024)} %param.20) | copy-start | bytes 12292
  283.8 10.1 %all-to-all-start = ((f32[1,8,64]{1,0,2:T(1,128)}), f32[1,8,64]{1,0,2:T(1,128)S(1)}, u32[]{:S(2)}, u32[]{:S(2)}) async-start(f32[1,8,64]{1,0,2:T(1,128)} %bitcast.3), calls=%async_computation | async-start | bytes 65536 | tf_op jit(solution)/shard_map/all_to_all | solution.py:100
  293.9 10.0 %all-to-all-start.2 = ((f32[1,8,64]{1,0,2:T(1,128)}), f32[1,8,64]{1,0,2:T(1,128)S(1)}, u32[]{:S(2)}, u32[]{:S(2)}) async-start(f32[1,8,64]{1,0,2:T(1,128)} %bitcast.21), calls=%async_computation.2 | async-start | bytes 65536 | tf_op jit(solution)/shard_map/all_to_all | solution.py:101
  303.9 12.1 %all-to-all-start.5 = ((f32[1,8,64]{1,0,2:T(1,128)}), f32[1,8,64]{1,0,2:T(1,128)S(1)}, u32[]{:S(2)}, u32[]{:S(2)}) async-start(f32[1,8,64]{1,0,2:T(1,128)} %bitcast.47), calls=%async_computation.6 | async-start | bytes 65536 | tf_op jit(solution)/shard_map/all_to_all | solution.py:101
  316.0 10.0 %all-to-all-start.3 = ((f32[1,8,64]{1,0,2:T(1,128)}), f32[1,8,64]{1,0,2:T(1,128)S(1)}, u32[]{:S(2)}, u32[]{:S(2)}) async-start(f32[1,8,64]{1,0,2:T(1,128)} %bitcast.30), calls=%async_computation.4 | async-start | bytes 65536 | tf_op jit(solution)/shard_map/all_to_all | solution.py:100
  325.9 11.6 %all-to-all-start.1 = ((f32[1,8,64,128]{3,1,0,2:T(8,128)}), f32[1,8,64,128]{3,1,0,2:T(8,128)S(1)}, u32[]{:S(2)}, u32[]{:S(2)}) async-start(f32[1,8,64,128]{3,1,0,2:T(8,128)} %copy.118), calls=%async_computation.1 | async-start | bytes 524288 | tf_op jit(solution)/shard_map/all_to_all | solution.py:104
  337.5 12.5 %all-to-all-start.4 = ((f32[1,8,64,128]{3,1,0,2:T(8,128)}), f32[1,8,64,128]{3,1,0,2:T(8,128)S(1)}, u32[]{:S(2)}, u32[]{:S(2)}) async-start(f32[1,8,64,128]{3,1,0,2:T(8,128)} %copy.131), calls=%async_computation.5 | async-start | bytes 524288 | tf_op jit(solution)/shard_map/all_to_all | solution.py:104
  340.9 72.5 %reduce-scatter.3.cloned.1.call-start = ((), (), s32[]{:S(2)}) async-start(), calls=%async_computation.10 | async-start | bytes 294912 | tf_op jit(solution)/shard_map/reduce_scatter | solution.py:130
  349.9 128.2 %reduce-scatter.5.cloned.1.call-start = ((), (), s32[]{:S(2)}) async-start(), calls=%async_computation.11 | async-start | bytes 294912 | tf_op jit(solution)/shard_map/reduce_scatter | solution.py:130
  350.1 129.3 %copy-start.1 = (s32[16]{0:T(128)S(1)}, s32[16]{0:T(128)}, u32[]{:S(2)}) copy-start(s32[16]{0:T(128)} %param.28) | copy-start | bytes 196
Sparse Core Ops, SparseCore 0:
  9.5 22.5 all-gather.4
  33.7 21.0 all-gather.6
  350.1 63.3 reduce-scatter.2
  416.6 61.4 reduce-scatter.4
where the time goes:
time: 487 us; the launch traced here: 486 us
  blocking collectives  222 us (46%)
  waiting for transfers between devices  143 us (29%)
  matrix products  49 us (10%)
  starting transfers between devices  22.4 us (5%)
  local copies, waits for them, and re-layouts  20.7 us (4%)
  other arithmetic  14.1 us (3%)
  between operations  14.1 us (3%)
    reduce_scatter x2, waiting for transfers between devices, local(): lax.psum_scatter(partial_out, 'tensor', scatter_dimension=1, tiled=True)  118 us
    all_gather x2, blocking collectives, local(): lax.all_gather(decode_inputs[step], 'tensor', axis=1, tiled=True)  62.9 us
    all_gather x2, blocking collectives, local(): lax.all_gather(kv_part, 'tensor', axis=1, tiled=True)  61.2 us
    all_gather x2, blocking collectives, local(): lax.all_gather(query_part, 'tensor', axis=1, tiled=True)  61.2 us
    psum x1, blocking collectives, local(): squares, head_dot = lax.psum((squares, head_dot), 'tensor')  37.1 us
    dot_general x2, matrix products, local(): partial_out = jnp.dot(attended, w_out, preferred_element_type=jnp.float32)  17.6 us
    dot_general x2, matrix products, local(): jnp.dot(normed, w_query, preferred_element_type=jnp.float32)  16.2 us
  transfers between devices with their start and end apart: 10, of which 7 were waited for; matrix products, arithmetic and copies ran while one was open for 14% of the time, Pallas kernels for 0%

commit v1 on v0

--- a/solution.py
+++ b/solution.py
@@ -73,7 +73,10 @@
         )
         kv_part = jnp.dot(normed, w_keyval, preferred_element_type=jnp.float32).astype(jnp.bfloat16)
         query_all, keyval = (
-            lax.all_gather(query_part, "tensor", axis=1, tiled=True),
+            jnp.concatenate(
+                lax.all_to_all(jnp.stack([query_part] * lax.axis_size("tensor")), "tensor", 0, 0),
+                axis=1,
+            ),
             lax.all_gather(kv_part, "tensor", axis=1, tiled=True),
         )
         query = query_all.reshape(rows, KVH, group, HD)

time: 487 us -> 447 us (0.918)
  blocking collectives: 222 us -> 162 us
  starting transfers between devices: 22.4 us -> 31.5 us
    all_gather x2 -> x0, blocking collectives: 61.2 us -> none  [local(): lax.all_gather(query_part, 'tensor', axis=1, tiled=True)]
    all_to_all x0 -> x2, starting transfers between devices: none -> 9.05 us  [local(): lax.all_to_all(jnp.stack([query_part] * lax.axis_size('tensor')), 'tensor...]
  transfers between devices with their start and end apart: 10 -> 12, of which waited for: 7 -> 8; matrix products, arithmetic and copies ran while one was open for 14% -> 19% of each run, Pallas kernels for 0% -> 0%
where the time goes in v1:
time: 447 us; the launch traced here: 445 us
  blocking collectives  162 us (36%)
  waiting for transfers between devices  147 us (33%)
  matrix products  53.4 us (12%)
  starting transfers between devices  31.5 us (7%)
  local copies, waits for them, and re-layouts  22 us (5%)
  other arithmetic  15.4 us (3%)
  between operations  14.1 us (3%)
    reduce_scatter x2, waiting for transfers between devices, local(): lax.psum_scatter(partial_out, 'tensor', scatter_dimension=1, tiled=True)  118 us
    all_gather x2, blocking collectives, local(): lax.all_gather(decode_inputs[step], 'tensor', axis=1, tiled=True)  63.4 us
    all_gather x2, blocking collectives, local(): lax.all_gather(kv_part, 'tensor', axis=1, tiled=True)  61.2 us
    psum x1, blocking collectives, local(): squares, head_dot = lax.psum((squares, head_dot), 'tensor')  37 us
    dot_general x2, matrix products, local(): partial_out = jnp.dot(attended, w_out, preferred_element_type=jnp.float32)  17.6 us
    dot_general x2, matrix products, local(): jnp.dot(normed, w_query, preferred_element_type=jnp.float32)  16.2 us
    all_to_all x2, waiting for transfers between devices, local(): lax.all_to_all(block_max[None], 'tensor', split_axis=2, concat_axis=0, ti...  9.28 us
    all_to_all x2, starting transfers between devices, local(): lax.all_to_all(jnp.stack([query_part] * lax.axis_size('tensor')), 'tensor...  9.05 us
  transfers between devices with their start and end apart: 12, of which 8 were waited for; matrix products, arithmetic and copies ran while one was open for 19% of the time, Pallas kernels for 0%

profile of v1, /device:TPU:0, one launch (start us, length us, event | category | flops | bytes accessed | tf_op | source)
XLA Modules:
  0.0 445.1 jit_solution(6229577311912191280)
XLA Ops:
  8.7 32.3 %all-gather = bf16[1,8,8192]{2,1,0:T(8,128)(2,1)S(1)} all-gather(bf16[1,8,1024]{2,1,0:T(8,128)(2,1)S(1)} %get-tuple-element.26), channel_id=2, replica_groups=mesh['groups'=2,'dp'=2,'tensor'=8] {'tensor'}, dimensions={2}, use_global_device_ids=true | all-gather | bytes 147456 | tf_op jit(solution)/shard_map/all_gather | solution.py:65
  41.2 3.5 convolution_convert_fusion.3
  44.8 30.6 %all_gather.20 = bf16[8,2048]{1,0:T(8,128)(2,1)S(1)} all-gather(bf16[8,256]{1,0:T(8,128)(2,1)S(1)} %convolution_convert_fusion.3), channel_id=1, replica_groups=mesh['groups'=2,'dp'=2,'tensor'=8] {'tensor'}, dimensions={1}, use_global_device_ids=true | all-gather | bytes 36864 | tf_op jit(solution)/shard_map/all_gather | solution.py:80
  76.0 8.2 %fusion.61 = (f32[8,8]{0,1:T(8,128)S(1)}, bf16[8,1024]{1,0:T(8,128)(2,1)S(1)}) fusion(bf16[8,8,128]{2,1,0:T(8,128)(2,1)S(1)} %gather_fusion.2, pred[8]{0:T(512)(128)(4,1)S(1)} %compare_and_fusion, bf16[8192,1024]{1,0:T(8,128)(2,1)} %param.23, bf16[1,8,8192]{2,1,0:T(8,128)(2,1)S(1)} %all-gather, f32[8192]{0:T(1024)S(1)} %copy-done.2, f32[8]{0:T(128)S(1)} %add_rsqrt_fusion.1), kind=kOutput, calls=%fused_computation.80 | convolution fusion | flops 134528960 | bytes 16974120 | tf_op jit(solution)/shard_map/dot_general | solution.py:71
  84.8 5.5 %all-to-all-start = ((bf16[8,8,1024]{2,1,0:T(8,128)(2,1)}), bf16[8,8,1024]{2,1,0:T(8,128)(2,1)S(1)}, u32[]{:S(2)}, u32[]{:S(2)}) async-start(bf16[8,8,1024]{2,1,0:T(8,128)(2,1)} %stack.14), calls=%async_computation | async-start | bytes 262144 | tf_op jit(solution)/shard_map/all_to_all | solution.py:77
  91.0 31.1 %all-gather.1 = bf16[1,8,8192]{2,1,0:T(8,128)(2,1)S(1)} all-gather(bf16[1,8,1024]{2,1,0:T(8,128)(2,1)S(1)} %get-tuple-element.27), channel_id=3, replica_groups=mesh['groups'=2,'dp'=2,'tensor'=8] {'tensor'}, dimensions={2}, use_global_device_ids=true | all-gather | bytes 147456 | tf_op jit(solution)/shard_map/all_gather | solution.py:65
  125.1 30.6 %all_gather.23 = bf16[8,2048]{1,0:T(8,128)(2,1)S(1)} all-gather(bf16[8,256]{1,0:T(8,128)(2,1)S(1)} %convolution_convert_fusion.2), channel_id=1, replica_groups=mesh['groups'=2,'dp'=2,'tensor'=8] {'tensor'}, dimensions={1}, use_global_device_ids=true | all-gather | bytes 36864 | tf_op jit(solution)/shard_map/all_gather | solution.py:80
  157.0 8.1 %convolution_convert_fusion = bf16[8,1024]{1,0:T(8,128)(2,1)S(1)} fusion(bf16[8192,1024]{1,0:T(8,128)(2,1)} %param.23, bf16[1,8,8192]{2,1,0:T(8,128)(2,1)S(1)} %all-gather.1, f32[8]{0:T(128)S(1)} %add_rsqrt_fusion, f32[8192]{0:T(1024)S(1)} %copy-done.2), kind=kOutput, calls=%fused_computation.31 | convolution fusion | flops 134488064 | bytes 16957472 | tf_op jit(solution)/shard_map/dot_general | solution.py:71
  166.5 3.6 fusion.1
  170.2 37.0 %all-reduce = (f32[8,256]{1,0:T(8,128)S(1)}, f32[8,256]{1,0:T(8,128)S(1)}) all-reduce(f32[8,256]{1,0:T(8,128)S(1)} %get-tuple-element.6, f32[8,256]{1,0:T(8,128)S(1)} %get-tuple-element.4), channel_id=1, replica_groups=mesh['groups'=2,'dp'=2,'tensor'=8] {'tensor'}, use_global_device_ids=true, to_apply=%region_1.0 | all-reduce | flops 4096 | bytes 32768 | tf_op jit(solution)/shard_map/psum | solution.py:39
  207.5 6.1 %gather_fusion.1 = bf16[8,256,1024]{2,1,0:T(8,128)(2,1)} fusion(bf16[16,256,1024]{2,1,0:T(8,128)(2,1)} %all-gather.5.cloned.1.call-done, s32[1024]{0:T(1024)S(1)} %pad_clamp_fusion.1), kind=kCustom, calls=%fused_computation.clone | custom fusion | bytes 8388640 | tf_op jit(solution)/shard_map/jit(_take)/gather | solution.py:49
  213.6 6.2 %gather_fusion.3 = bf16[8,256,1024]{2,1,0:T(8,128)(2,1)} fusion(bf16[16,256,1024]{2,1,0:T(8,128)(2,1)} %all-gather.7.cloned.1.call-done, s32[1024]{0:T(1024)S(1)} %pad_clamp_fusion.1), kind=kCustom, calls=%fused_computation.3.clone | custom fusion | bytes 8388640 | tf_op jit(solution)/shard_map/jit(_take)/gather | solution.py:50
  219.8 7.5 %select_bitcast_fusion.1 = (bf16[8,32,8,8,128]{4,3,2,1,0:T(8,128)(2,1)}, bf16[8,32,8,8,128]{4,3,2,1,0:T(8,128)(2,1)}) fusion(bf16[8,256,1024]{2,1,0:T(8,128)(2,1)} %gather_fusion.1, pred[8]{0:T(512)(128)(4,1)S(1)} %get-tuple-element.18, bf16[8,256,1024]{2,1,0:T(8,128)(2,1)} %gather_fusion.3), kind=kLoop, calls=%fused_computation.20 | loop fusion | flops 4194304 | bytes 16777224
  227.9 3.5 all-to-all-start.4
  231.5 3.5 fusion.105
  234.9 3.8 all-to-all-done.4
  263.0 5.4 %all-to-all-start.7 = ((f32[1,8,64]{1,0,2:T(1,128)}), f32[1,8,64]{1,0,2:T(1,128)S(1)}, u32[]{:S(2)}, u32[]{:S(2)}) async-start(f32[1,8,64]{1,0,2:T(1,128)} %bitcast.47), calls=%async_computation.8 | async-start | bytes 65536 | tf_op jit(solution)/shard_map/all_to_all | solution.py:104
  268.5 6.6 %all-to-all-done.7 = f32[1,8,64]{1,0,2:T(1,128)S(1)} async-done(((f32[1,8,64]{1,0,2:T(1,128)}), f32[1,8,64]{1,0,2:T(1,128)S(1)}, u32[]{:S(2)}, u32[]{:S(2)}) %all-to-all-start.7) | async-done | bytes 2080 | tf_op jit(solution)/shard_map/all_to_all | solution.py:104
  278.4 6.6 %all-to-all-done.5 = f32[1,8,64]{1,0,2:T(1,128)S(1)} async-done(((f32[1,8,64]{1,0,2:T(1,128)}), f32[1,8,64]{1,0,2:T(1,128)S(1)}, u32[]{:S(2)}, u32[]{:S(2)}) %all-to-all-start.5) | async-done | bytes 2080 | tf_op jit(solution)/shard_map/all_to_all | solution.py:103
  288.8 7.8 %all-to-all-done.2 = f32[1,8,64,128]{3,1,0,2:T(8,128)S(1)} async-done(((f32[1,8,64,128]{3,1,0,2:T(8,128)}), f32[1,8,64,128]{3,1,0,2:T(8,128)S(1)}, u32[]{:S(2)}, u32[]{:S(2)}) %all-to-all-start.2) | async-done | bytes 262176 | tf_op jit(solution)/shard_map/all_to_all | solution.py:107
  300.2 8.8 %fusion.75 = f32[8,8192]{1,0:T(8,128)} fusion(bf16[1024,8192]{1,0:T(8,128)(2,1)} %param.25, f32[8,8,128]{2,1,0:T(8,128)S(1)} %fusion.44, bf16[8,8,128]{2,1,0:T(8,128)(2,1)S(1)} %gather_fusion.4, f32[8,8]{0,1:T(8,128)S(1)} %copy.121, f32[8,8]{0,1:T(8,128)S(1)} %copy.118, f32[8,8]{0,1:T(8,128)S(1)} %copy.117, f32[8,8]{0,1:T(8,128)S(1)} %copy.112, ...), kind=kOutput, calls=%fused_computation.98 | convolution fusion | flops 134283264 | bytes 17089544 | tf_op jit(solution)/shard_map/dot_general | solution.py:132
  309.3 8.8 %fusion.73 = f32[8,8192]{1,0:T(8,128)} fusion(bf16[1024,8192]{1,0:T(8,128)(2,1)} %param.25, f32[8,8,1,128]{3,2,1,0:T(1,128)S(1)} %fusion.63, f32[8,8,128]{2,0,1:T(8,128)S(1)} %multiply_reduce_fusion, f32[8,8]{0,1:T(8,128)S(1)} %get-tuple-element.13, f32[8,8]{0,1:T(8,128)S(1)} %get-tuple-element.15, f32[8,8]{0,1:T(8,128)S(1)} %get-tuple-element.14), kind=kOutput, calls=%fused_computation.96 | convolution fusion | flops 134258688 | bytes 17105664 | tf_op jit(solution)/shard_map/dot_general | solution.py:132
  318.7 53.8 %reduce-scatter.3.cloned.1.call-done = f32[8,1024]{1,0:T(8,128)} async-done(((f32[8,8192]{1,0:T(8,128)}), f32[8,1024]{1,0:T(8,128)}) %reduce-scatter.3.cloned.1.call-update) | async-done | bytes 32784 | tf_op jit(solution)/shard_map/reduce_scatter | solution.py:133
  373.3 63.9 %reduce-scatter.5.cloned.1.call-done = f32[8,1024]{1,0:T(8,128)} async-done(((f32[8,8192]{1,0:T(8,128)}), f32[8,1024]{1,0:T(8,128)}) %reduce-scatter.5.cloned.1.call-update) | async-done | bytes 32784 | tf_op jit(solution)/shard_map/reduce_scatter | solution.py:133
  (97 shorter events, 48.2 us)
Async XLA Ops:
  7.2 158.7 %copy-start = (s32[16]{0:T(128)S(1)}, s32[16]{0:T(128)}, u32[]{:S(2)}) copy-start(s32[16]{0:T(128)} %param.28) | copy-start | bytes 196
  7.2 1.5 copy-start.3
  7.2 34.0 %copy-start.2 = (f32[8192]{0:T(1024)S(1)}, f32[8192]{0:T(1024)}, u32[]{:S(2)}) copy-start(f32[8192]{0:T(1024)} %param.22) | copy-start | bytes 98308
  7.2 200.3 %all-gather.5.cloned.1.call-start = ((), (), s32[]{:S(2)}) async-start(), calls=%async_computation.10 | async-start | bytes 12582912 | tf_op jit(solution)/shard_map/all_gather | solution.py:46
  7.9 205.7 %all-gather.7.cloned.1.call-start = ((), (), s32[]{:S(2)}) async-start(), calls=%async_computation.11 | async-start | bytes 12582912 | tf_op jit(solution)/shard_map/all_gather | solution.py:47
  84.8 142.4 %all-to-all-start = ((bf16[8,8,1024]{2,1,0:T(8,128)(2,1)}), bf16[8,8,1024]{2,1,0:T(8,128)(2,1)S(1)}, u32[]{:S(2)}, u32[]{:S(2)}) async-start(bf16[8,8,1024]{2,1,0:T(8,128)(2,1)} %stack.14), calls=%async_computation | async-start | bytes 262144 | tf_op jit(solution)/shard_map/all_to_all | solution.py:77
  157.0 8.8 %copy-start.6 = (s32[16]{0:T(128)S(1)}, s32[16]{0:T(128)}, u32[]{:S(2)}) copy-start(s32[16]{0:T(128)} %param.29) | copy-start | bytes 196
  157.0 9.5 %copy-start.4 = (f32[1024]{0:T(1024)S(1)}, f32[1024]{0:T(1024)}, u32[]{:S(2)}) copy-start(f32[1024]{0:T(1024)} %param.19) | copy-start | bytes 12292
  157.0 9.5 %copy-start.5 = (f32[1024]{0:T(1024)S(1)}, f32[1024]{0:T(1024)}, u32[]{:S(2)}) copy-start(f32[1024]{0:T(1024)} %param.20) | copy-start | bytes 12292
  227.9 10.8 %all-to-all-start.4 = ((bf16[8,8,1024]{2,1,0:T(8,128)(2,1)}), bf16[8,8,1024]{2,1,0:T(8,128)(2,1)S(1)}, u32[]{:S(2)}, u32[]{:S(2)}) async-start(bf16[8,8,1024]{2,1,0:T(8,128)(2,1)} %stack.16), calls=%async_computation.5 | async-start | bytes 262144 | tf_op jit(solution)/shard_map/all_to_all | solution.py:77
  242.9 10.1 %all-to-all-start.1 = ((f32[1,8,64]{1,0,2:T(1,128)}), f32[1,8,64]{1,0,2:T(1,128)S(1)}, u32[]{:S(2)}, u32[]{:S(2)}) async-start(f32[1,8,64]{1,0,2:T(1,128)} %bitcast.3), calls=%async_computation.1 | async-start | bytes 65536 | tf_op jit(solution)/shard_map/all_to_all | solution.py:103
  253.0 10.0 %all-to-all-start.3 = ((f32[1,8,64]{1,0,2:T(1,128)}), f32[1,8,64]{1,0,2:T(1,128)S(1)}, u32[]{:S(2)}, u32[]{:S(2)}) async-start(f32[1,8,64]{1,0,2:T(1,128)} %bitcast.21), calls=%async_computation.3 | async-start | bytes 65536 | tf_op jit(solution)/shard_map/all_to_all | solution.py:104
  263.0 12.1 %all-to-all-start.7 = ((f32[1,8,64]{1,0,2:T(1,128)}), f32[1,8,64]{1,0,2:T(1,128)S(1)}, u32[]{:S(2)}, u32[]{:S(2)}) async-start(f32[1,8,64]{1,0,2:T(1,128)} %bitcast.47), calls=%async_computation.8 | async-start | bytes 65536 | tf_op jit(solution)/shard_map/all_to_all | solution.py:104
  275.1 10.0 %all-to-all-start.5 = ((f32[1,8,64]{1,0,2:T(1,128)}), f32[1,8,64]{1,0,2:T(1,128)S(1)}, u32[]{:S(2)}, u32[]{:S(2)}) async-start(f32[1,8,64]{1,0,2:T(1,128)} %bitcast.30), calls=%async_computation.6 | async-start | bytes 65536 | tf_op jit(solution)/shard_map/all_to_all | solution.py:103
  285.0 11.6 %all-to-all-start.2 = ((f32[1,8,64,128]{3,1,0,2:T(8,128)}), f32[1,8,64,128]{3,1,0,2:T(8,128)S(1)}, u32[]{:S(2)}, u32[]{:S(2)}) async-start(f32[1,8,64,128]{3,1,0,2:T(8,128)} %copy.114), calls=%async_computation.2 | async-start | bytes 524288 | tf_op jit(solution)/shard_map/all_to_all | solution.py:107
  296.6 12.5 %all-to-all-start.6 = ((f32[1,8,64,128]{3,1,0,2:T(8,128)}), f32[1,8,64,128]{3,1,0,2:T(8,128)S(1)}, u32[]{:S(2)}, u32[]{:S(2)}) async-start(f32[1,8,64,128]{3,1,0,2:T(8,128)} %copy.127), calls=%async_computation.7 | async-start | bytes 524288 | tf_op jit(solution)/shard_map/all_to_all | solution.py:107
  300.0 72.5 %reduce-scatter.3.cloned.1.call-start = ((), (), s32[]{:S(2)}) async-start(), calls=%async_computation.12 | async-start | bytes 294912 | tf_op jit(solution)/shard_map/reduce_scatter | solution.py:133
  309.0 128.2 %reduce-scatter.5.cloned.1.call-start = ((), (), s32[]{:S(2)}) async-start(), calls=%async_computation.13 | async-start | bytes 294912 | tf_op jit(solution)/shard_map/reduce_scatter | solution.py:133
  309.2 129.4 %copy-start.1 = (s32[16]{0:T(128)S(1)}, s32[16]{0:T(128)}, u32[]{:S(2)}) copy-start(s32[16]{0:T(128)} %param.28) | copy-start | bytes 196
Sparse Core Ops, SparseCore 0:
  9.5 22.5 all-gather.4
  33.7 21.0 all-gather.6
  309.2 63.3 reduce-scatter.2
  375.7 61.4 reduce-scatter.4
